TPU v7x, 256 devices: a whole 4x4x8 slice. The times are simulated.
256 devices in a mesh: seq: 64 (over z, y, core), chan: 4 (over x).
Axes of the slice: x: 4, y: 4, z: 8, core: 2. Of those that a mesh axis runs over, the one named last changes fastest.
Arguments:
- signal: bfloat16 [16384, 2048], P('seq', 'chan'), may hold values from -6 to 6
- gate_rows: bfloat16 [16384, 2048], P('seq', 'chan'), may hold values from -60 to 60
- skip_gain: float32 [2048], P('chan'), may hold values from 0.5 to 1.5
- filter_taps: bfloat16 [16384, 16], P(None, 'chan'), may hold values from -2 to 2
- queries: bfloat16 [16384, 2048], P('seq', 'chan'), may hold values from -6 to 6
- key_rows: bfloat16 [16384, 2048], P('seq', 'chan'), may hold values from -6 to 6
Outputs:
- conv_mixed: bfloat16 [16384, 2048], P('seq', 'chan')
- attended: bfloat16 [256, 1024, 128], P(('chan', 'seq'))
All inputs are finite; a program needn't handle non-finite values.
Results may differ from a plain program's by a relative error of at most 0.0061.
Values may be sent and summed in bfloat16 or wider, within the bound.
A program may use at most 128 MiB of HBM per device.

v0:
```python
import math
import jax
import jax.numpy as jnp
from jax import lax
from jax.sharding import PartitionSpec as P


def toeplitz_block(padded_taps, out_start, in_start, block_rows, group_rows, seq_len):
    heads_loc = padded_taps.shape[0]
    window_len = group_rows + block_rows - 1
    offset = out_start - in_start - block_rows + 1 + seq_len
    window = lax.dynamic_slice_in_dim(padded_taps, offset, window_len, 1)
    flipped = jnp.concatenate(
        [window[:, ::-1], jnp.zeros((heads_loc, 1), padded_taps.dtype)], axis=1
    )
    repeated = jnp.tile(flipped, (1, group_rows))[:, : group_rows * window_len]
    return repeated.reshape(heads_loc, group_rows, window_len)[:, :, group_rows - 1 :]


def add_range(total_acc, inputs, first_row, target, lower, upper, padded_taps, seq_len, head_dim):
    block_rows = inputs.shape[0]
    group_rows = total_acc.shape[0]
    positions = first_row + jnp.arange(block_rows, dtype=jnp.int32)
    keep_rows = (positions >= lower) & (positions < upper)
    is_live = (first_row < upper) & (first_row + block_rows > lower)

    def compute(running):
        masked = jnp.where(keep_rows[:, None], inputs, jnp.zeros_like(inputs))
        matrix = toeplitz_block(padded_taps, target, first_row, block_rows, group_rows, seq_len)
        heads_loc = matrix.shape[0]
        split_in = masked.reshape(block_rows, heads_loc, head_dim)
        product = jnp.einsum("htn,nhd->thd", matrix, split_in, preferred_element_type=jnp.float32)
        return running + product.reshape(group_rows, heads_loc * head_dim)

    def unchanged(running):
        return running

    return lax.cond(is_live, compute, unchanged, total_acc)


def attend_block(q_rows, q_pos, key_end, keys_all, values_all, score_scale):
    key_part = keys_all[:key_end]
    value_part = values_all[:key_end]
    raw_scores = (
        jnp.einsum("qd,kd->qk", q_rows, key_part, preferred_element_type=jnp.float32) * score_scale
    )
    k_pos = jnp.arange(key_end, dtype=jnp.int32)
    masked = jnp.where(k_pos[None, :] <= q_pos[:, None], raw_scores, -jnp.inf)
    peak = jnp.max(masked, axis=1)
    exp_scores = jnp.exp(masked - peak[:, None])
    row_total = jnp.sum(exp_scores, axis=1)
    weighted = jnp.dot(
        exp_scores.astype(jnp.bfloat16), value_part, preferred_element_type=jnp.float32
    )
    return (weighted / row_total[:, None]).astype(jnp.bfloat16)


def shards(signal, gate_rows, skip_gain, filter_taps, queries, key_rows):
    group_rows, local_width = signal.shape
    heads_loc = filter_taps.shape[1]
    head_dim = local_width // heads_loc
    seq_count = lax.axis_size("seq")
    chan_count = lax.axis_size("chan")
    my_group = lax.axis_index("seq")
    seq_len = group_rows * seq_count
    padded_taps = jnp.concatenate(
        [jnp.zeros((seq_len, heads_loc), filter_taps.dtype), filter_taps], axis=0
    ).T
    own_start = my_group * group_rows
    own_upper = own_start + group_rows
    halfway = seq_count // 2
    own_lower = jnp.zeros((), jnp.int32)
    help_upper = jnp.zeros((), jnp.int32)
    help_start = (my_group + halfway) % seq_count * group_rows

    def add_both(totals, inputs, first_row):
        own_acc = add_range(
            totals[0],
            inputs,
            first_row,
            own_start,
            own_lower,
            own_upper,
            padded_taps,
            seq_len,
            head_dim,
        )
        help_acc = add_range(
            totals[1], inputs, first_row, help_start, 0, help_upper, padded_taps, seq_len, head_dim
        )
        return (own_acc, help_acc)

    zero_acc = jnp.zeros((group_rows, local_width), jnp.float32)
    totals = (zero_acc, zero_acc)
    incoming = lax.all_gather(signal, "seq", axis=0, tiled=True)
    incoming_rows = incoming.shape[0]
    pieces_count = incoming_rows // group_rows
    blocks = incoming.reshape(pieces_count, group_rows, local_width)
    starts = group_rows * jnp.arange(pieces_count, dtype=jnp.int32)

    def step_block(running, entry_pair):
        return (add_both(running, entry_pair[0], entry_pair[1]), None)

    totals, unused = lax.scan(step_block, totals, (blocks, starts))
    own_acc, help_acc = totals
    conv_mixed = (
        gate_rows.astype(jnp.float32) * (own_acc + skip_gain[None, :] * signal.astype(jnp.float32))
    ).astype(jnp.bfloat16)
    widened = conv_mixed.astype(jnp.float32)
    squares = jnp.sum(jnp.square(widened), axis=1)
    whole_sum = lax.psum(squares, "chan")
    inv_scale = lax.rsqrt(whole_sum / (local_width * chan_count) + 1e-06)
    values = (widened * inv_scale[:, None]).astype(jnp.bfloat16)
    query_sets = seq_count // heads_loc
    query_rows = group_rows // query_sets
    query_send = (
        queries.reshape(query_sets, query_rows, heads_loc, head_dim)
        .transpose(2, 0, 1, 3)
        .reshape(seq_count, query_rows, head_dim)
    )
    pair_stack = jnp.concatenate(
        [
            key_rows.reshape(group_rows, heads_loc, head_dim),
            values.reshape(group_rows, heads_loc, head_dim),
        ],
        axis=2,
    ).transpose(1, 0, 2)
    pair_send = jnp.broadcast_to(
        pair_stack[:, None], (heads_loc, query_sets, group_rows, 2 * head_dim)
    ).reshape(seq_count, group_rows, 2 * head_dim)
    query_got, pair_got = (
        lax.all_to_all(query_send, "seq", split_axis=0, concat_axis=1, tiled=True),
        lax.all_to_all(pair_send, "seq", split_axis=0, concat_axis=1, tiled=True),
    )
    query_all = query_got[0]
    keys_all = pair_got[0, :, :head_dim]
    values_all = pair_got[0, :, head_dim:]
    my_set = my_group % query_sets
    query_len = query_all.shape[0]
    query_block = min(512, query_len)
    score_scale = 1.0 / math.sqrt(head_dim)
    outputs = []
    for query_step in range(query_len // query_block):
        local_index = query_step * query_block + jnp.arange(query_block, dtype=jnp.int32)
        q_pos = (
            local_index // query_rows * group_rows + my_set * query_rows + local_index % query_rows
        )
        last_source = ((query_step + 1) * query_block - 1) // query_rows
        key_end = (last_source + 1) * group_rows
        q_rows = query_all[query_step * query_block : (query_step + 1) * query_block]
        outputs.append(attend_block(q_rows, q_pos, key_end, keys_all, values_all, score_scale))
    attended = jnp.concatenate(outputs, axis=0)[None]
    return (conv_mixed, attended)


def solution(mesh):
    in_specs = (
        P("seq", "chan"),
        P("seq", "chan"),
        P("chan"),
        P(None, "chan"),
        P("seq", "chan"),
        P("seq", "chan"),
    )
    out_specs = (P("seq", "chan"), P(("chan", "seq"), None, None))
    return jax.shard_map(shards, mesh=mesh, in_specs=in_specs, out_specs=out_specs, check_vma=False)
```

profile of v0, /device:TPU:8, one launch (start us, length us, event | category | flops | bytes accessed | tf_op | source)
XLA Modules:
  0.0 989.2 jit_solution(6087917328609244170)
XLA Ops:
  7.2 0.7 all-gather.2.cloned.1.call-update
  7.9 1.0 reshape.122
  8.9 0.7 copy.16
  9.7 12.1 %all-to-all-start.1 = ((bf16[64,16,128]{2,1,0:T(8,128)(2,1)}), bf16[64,16,128]{2,1,0:T(8,128)(2,1)S(1)}, u32[]{:S(2)}, u32[]{:S(2)}) async-start(bf16[64,16,128]{2,1,0:T(8,128)(2,1)} %bitcast.11), calls=%async_computation.1 | async-start | bytes 524288 | tf_op jit(solution)/shard_map/all_to_all | solution.py:132
  21.8 1.7 reshape.119
  23.5 1.7 pad_bitcast_fusion
  25.2 86.5 %all-gather.2.cloned.1.call-done = bf16[16384,512]{1,0:T(8,128)(2,1)} async-done(((bf16[256,512]{1,0:T(8,128)(2,1)}), bf16[16384,512]{1,0:T(8,128)(2,1)}) %all-gather.2.cloned.1.call-update) | async-done | bytes 16777232 | tf_op jit(solution)/shard_map/all_gather | solution.py:95
  111.7 22.3 %copy.13 = bf16[64,256,512]{1,2,0:T(8,128)(2,1)} copy(bf16[64,256,512]{2,1,0:T(8,128)(2,1)} %bitcast.58) | data formatting | bytes 33554432 | tf_op jit(solution)/shard_map/while | solution.py:104
  134.1 142.4 %while.13 = (s32[]{:T(128)}, f32[256,512]{0,1:T(8,128)S(1)}, s32[64]{0:T(128)S(1)}, s32[]{:T(128)}, bf16[64,256,512]{1,2,0:T(8,128)(2,1)}, /*index=5*/s32[]{:T(1...) while((s32[]{:T(128)}, f32[256,512]{0,1:T(8,128)S(1)}, s32[64]{0:T(128)S(1)}, s32[]{:T(128)}, ...), condition=%wide.region_3.4_spmd, body=%wide.region_0.3_spmd.sunk | while | flops 67372048 | bytes 10779659 | solution.py:104
  135.9 7.0 conditional.2
  137.2 0.8 constant_dynamic-slice_fusion
  138.4 1.0 constant_dynamic-slice_fusion.1
  139.5 0.8 copy.17
  140.7 1.8 reshape.110
  143.0 0.6 dynamic_slice.18
  144.8 7.0 conditional.2
  146.1 0.8 constant_dynamic-slice_fusion
  147.3 1.0 constant_dynamic-slice_fusion.1
  148.4 0.8 copy.17
  149.5 1.8 reshape.110
  153.7 7.0 conditional.2
  154.9 0.8 constant_dynamic-slice_fusion
  156.2 1.0 constant_dynamic-slice_fusion.1
  157.2 0.8 copy.17
  158.4 1.8 reshape.110
  160.7 0.6 dynamic_slice.18
  162.6 0.6 dynamic_slice.18
  166.4 0.6 dynamic_slice.18
  168.3 0.6 dynamic_slice.18
  170.2 0.6 dynamic_slice.18
  174.0 0.6 dynamic_slice.18
  175.9 0.6 dynamic_slice.18
  181.6 0.6 dynamic_slice.18
  183.5 0.6 dynamic_slice.18
  187.3 0.6 dynamic_slice.18
  276.7 1.2 fusion.28
  277.9 10.4 %psum.7 = f32[256]{0:T(256)S(1)} all-reduce(f32[256]{0:T(256)S(1)} %get-tuple-element.129), channel_id=1, replica_groups=mesh['seq'=64,'chan'=4] {'chan'}, use_global_device_ids=true, to_apply=%region_5.6 | all-reduce | flops 256 | bytes 2048 | tf_op jit(solution)/shard_map/psum | solution.py:111
  288.5 1.2 maximum_bitcast_fusion
  289.8 4.2 broadcast_in_dim.23
  294.0 429.0 %all-to-all-start = ((bf16[64,256,256]{2,1,0:T(8,128)(2,1)}), bf16[64,256,256]{2,1,0:T(8,128)(2,1)}, u32[]{:S(2)}, u32[]{:S(2)}) async-start(bf16[64,256,256]{2,1,0:T(8,128)(2,1)} %bitcast.56), calls=%async_computation | async-start | bytes 16777216 | tf_op jit(solution)/shard_map/all_to_all | solution.py:133
  723.1 186.1 %all-to-all-done = bf16[64,256,256]{2,1,0:T(8,128)(2,1)} async-done(((bf16[64,256,256]{2,1,0:T(8,128)(2,1)}), bf16[64,256,256]{2,1,0:T(8,128)(2,1)}, u32[]{:S(2)}, u32[]{:S(2)}) %all-to-all-start) | async-done | bytes 8388640 | tf_op jit(solution)/shard_map/all_to_all | solution.py:133
  909.2 9.2 fusion.47
  918.4 8.0 fusion.11
  926.4 8.8 fusion.25
  935.2 16.5 %fusion.46 = (f32[512]{0:T(512)S(1)}, f32[512,16384]{0,1:T(8,128)}) fusion(bf16[512,128]{1,0:T(8,128)(2,1)S(1)} %bitcast.61, bf16[1,16384,256]{2,1,0:T(8,128)(2,1)} %bitcast.8, s32[512]{0:T(512)S(1)} %get-tuple-element.138), kind=kOutput, calls=%fused_computation.70 | convolution fusion | flops 2181037568 | bytes 37883904 | tf_op jit(solution)/shard_map/qd,kd->qk/dot_general | solution.py:45
  951.7 15.0 %fusion.6 = f32[512]{0:T(512)S(1)} fusion(f32[512,16384]{0,1:T(8,128)} %get-tuple-element.134, f32[512]{0:T(512)S(1)} %get-tuple-element.133), kind=kLoop, calls=%fused_computation.14 | loop fusion | flops 16776704 | bytes 33558528 | tf_op jit(solution)/shard_map/reduce_sum | solution.py:51
  966.8 14.9 %fusion.19 = bf16[512,128]{1,0:T(8,128)(2,1)S(1)} fusion(bf16[1,16384,256]{2,1,0:T(8,128)(2,1)} %bitcast.8, f32[512,16384]{0,1:T(8,128)} %get-tuple-element.134, f32[512]{0:T(512)S(1)} %get-tuple-element.133, f32[512]{0:T(512)S(1)} %fusion.6), kind=kOutput, calls=%fused_computation.30 | convolution fusion | flops 2164391936 | bytes 37883904 | tf_op jit(solution)/shard_map/dot_general | solution.py:52
  981.7 0.7 maximum_bitcast_fusion.1
  (219 shorter events, 40.4 us)
Async XLA Ops:
  7.2 104.5 %all-gather.2.cloned.1.call-start = ((), (), s32[]{:S(2)}) async-start(), calls=%async_computation.2 | async-start | bytes 17039360 | tf_op jit(solution)/shard_map/all_gather | solution.py:95
  9.7 280.1 %all-to-all-start.1 = ((bf16[64,16,128]{2,1,0:T(8,128)(2,1)}), bf16[64,16,128]{2,1,0:T(8,128)(2,1)S(1)}, u32[]{:S(2)}, u32[]{:S(2)}) async-start(bf16[64,16,128]{2,1,0:T(8,128)(2,1)} %bitcast.11), calls=%async_computation.1 | async-start | bytes 524288 | tf_op jit(solution)/shard_map/all_to_all | solution.py:132
  134.0 142.6 %copy-start = (bf16[256,512]{1,0:T(8,128)(2,1)S(1)}, bf16[256,512]{1,0:T(8,128)(2,1)}, u32[]{:S(2)}) copy-start(bf16[256,512]{1,0:T(8,128)(2,1)} %param.10) | copy-start | bytes 786436
  134.1 142.6 %copy-start.2 = (f32[512]{0:T(512)S(1)}, f32[512]{0:T(512)}, u32[]{:S(2)}) copy-start(f32[512]{0:T(512)} %param.12) | copy-start | bytes 6148
  277.9 640.5 %copy-start.1 = (bf16[256,512]{1,0:T(8,128)(2,1)}, bf16[256,512]{1,0:T(8,128)(2,1)S(1)}, u32[]{:S(2)}) copy-start(bf16[256,512]{1,0:T(8,128)(2,1)S(1)} %get-tuple-element.130) | copy-start | bytes 786436
  294.0 615.1 %all-to-all-start = ((bf16[64,256,256]{2,1,0:T(8,128)(2,1)}), bf16[64,256,256]{2,1,0:T(8,128)(2,1)}, u32[]{:S(2)}, u32[]{:S(2)}) async-start(bf16[64,256,256]{2,1,0:T(8,128)(2,1)} %bitcast.56), calls=%async_computation | async-start | bytes 16777216 | tf_op jit(solution)/shard_map/all_to_all | solution.py:133
Sparse Core Ops, SparseCore 0:
  10.7 100.8 all-gather.1
where the time goes:
time: 997 us; the launch traced here: 989 us
  starting transfers between devices  441 us (44%)
  waiting for transfers between devices  273 us (27%)
  local copies, waits for them, and re-layouts  87.6 us (9%)
  loops' own time  83.6 us (8%)
  matrix products  50.6 us (5%)
  other arithmetic  28.5 us (3%)
  between operations  14.2 us (1%)
  blocking collectives  10.4 us (1%)
    all_to_all x1, starting transfers between devices, shards(): lax.all_to_all(pair_send, 'seq', split_axis=0, concat_axis=1, tiled=True)  429 us
    all_to_all x1, waiting for transfers between devices, shards(): lax.all_to_all(pair_send, 'seq', split_axis=0, concat_axis=1, tiled=True)  186 us
    all_gather x1, waiting for transfers between devices, shards(): incoming = lax.all_gather(signal, 'seq', axis=0, tiled=True)  86.5 us
    another operation x1, loops' own time, shards(): totals, unused = lax.scan(step_block, totals, (blocks, starts))  80.7 us
    dynamic_slice x67, local copies, waits for them, and re-layouts, shards(): totals, unused = lax.scan(step_block, totals, (blocks, starts))  42.6 us
    dot_general x2, matrix products, attend_block(): jnp.einsum('qd,kd->qk', q_rows, key_part, preferred_element_type=jnp.floa...  25.7 us
    dot_general x2, matrix products, attend_block(): jnp.dot(exp_scores.astype(jnp.bfloat16), value_part, preferred_element_ty...  23.7 us
    reduce_sum x2, other arithmetic, attend_block(): row_total = jnp.sum(exp_scores, axis=1)  23.1 us
  transfers between devices with their start and end apart: 3, of which 2 were waited for; matrix products, arithmetic and copies ran while one was open for 9% of the time, Pallas kernels for 0%

commit v1 on v0

--- a/solution.py
+++ b/solution.py
@@ -92,7 +92,15 @@
 
     zero_acc = jnp.zeros((group_rows, local_width), jnp.float32)
     totals = (zero_acc, zero_acc)
-    incoming = lax.all_gather(signal, "seq", axis=0, tiled=True)
+    incoming = jnp.concatenate(
+        lax.all_to_all(
+            jnp.stack([signal for _ in range(lax.axis_size("seq"))], axis=0),
+            axis_name="seq",
+            split_axis=0,
+            concat_axis=0,
+        ),
+        axis=0,
+    )
     incoming_rows = incoming.shape[0]
     pieces_count = incoming_rows // group_rows
     blocks = incoming.reshape(pieces_count, group_rows, local_width)

time: 997 us -> 1260 us (1.26)
  waiting for transfers between devices: 273 us -> 552 us
  local copies, waits for them, and re-layouts: 87.6 us -> 68.2 us
  starting transfers between devices: 441 us -> 456 us
  between operations: 14.2 us -> 0.82 us
    all_to_all x0 -> x1, waiting for transfers between devices: none -> 366 us  [shards(): lax.all_to_all(jnp.stack([signal for _ in range(lax.axis_size('seq'))], a...]
    all_gather x1 -> x0, waiting for transfers between devices: 86.5 us -> none  [shards(): incoming = lax.all_gather(signal, 'seq', axis=0, tiled=True)]
    while x2 -> x1, local copies, waits for them, and re-layouts: 22.5 us -> 0.2 us  [shards(): totals, unused = lax.scan(step_block, totals, (blocks, starts))]
  transfers between devices with their start and end apart: 3 -> 3, of which waited for: 2 -> 2; matrix products, arithmetic and copies ran while one was open for 9% -> 5% of each run, Pallas kernels for 0% -> 0%
where the time goes in v1:
time: 1260 us; the launch traced here: 1250 us
  waiting for transfers between devices  552 us (44%)
  starting transfers between devices  456 us (36%)
  loops' own time  85 us (7%)
  local copies, waits for them, and re-layouts  68.2 us (5%)
  matrix products  50.6 us (4%)
  other arithmetic  28.5 us (2%)
    all_to_all x1, starting transfers between devices, shards(): lax.all_to_all(pair_send, 'seq', split_axis=0, concat_axis=1, tiled=True)  432 us
    all_to_all x1, waiting for transfers between devices, shards(): lax.all_to_all(jnp.stack([signal for _ in range(lax.axis_size('seq'))], a...  366 us
    all_to_all x1, waiting for transfers between devices, shards(): lax.all_to_all(pair_send, 'seq', split_axis=0, concat_axis=1, tiled=True)  186 us
    another operation x1, loops' own time, shards(): totals, unused = lax.scan(step_block, totals, (blocks, starts))  82.1 us
    dynamic_slice x67, local copies, waits for them, and re-layouts, shards(): totals, unused = lax.scan(step_block, totals, (blocks, starts))  41.1 us
    dot_general x2, matrix products, attend_block(): jnp.einsum('qd,kd->qk', q_rows, key_part, preferred_element_type=jnp.floa...  25.7 us
  transfers between devices with their start and end apart: 3, of which 2 were waited for; matrix products, arithmetic and copies ran while one was open for 5% of the time, Pallas kernels for 0%

profile of v1, /device:TPU:8, one launch (start us, length us, event | category | flops | bytes accessed | tf_op | source)
XLA Modules:
  0.0 1252.2 jit_solution(6473332468961747640)
XLA Ops:
  0.6 1.1 copy.14
  1.7 6.1 stack.2
  7.8 12.4 all-to-all-start
  20.3 0.8 copy.17
  21.1 0.8 reshape.117
  21.8 0.8 pad_bitcast_fusion
  22.6 366.4 %all-to-all-done = bf16[64,256,512]{1,2,0:T(8,128)(2,1)} async-done(((bf16[64,256,512]{1,2,0:T(8,128)(2,1)}), bf16[64,256,512]{1,2,0:T(8,128)(2,1)}, u32[]{:S(2)}, u32[]{:S(2)}) %all-to-all-start) | async-done | bytes 16777248 | tf_op jit(solution)/shard_map/all_to_all | solution.py:96
  389.0 11.5 all-to-all-start.2
  400.6 142.4 %while.13 = (s32[]{:T(128)}, f32[256,512]{0,1:T(8,128)S(1)}, s32[64]{0:T(128)S(1)}, s32[]{:T(128)}, bf16[64,256,512]{1,2,0:T(8,128)(2,1)}, /*index=5*/s32[]{:T(1...) while((s32[]{:T(128)}, f32[256,512]{0,1:T(8,128)S(1)}, s32[64]{0:T(128)S(1)}, s32[]{:T(128)}, ...), condition=%wide.region_3.4_spmd, body=%wide.region_0.3_spmd.sunk | while | flops 67372048 | bytes 10779659 | solution.py:112
  400.6 0.6 dynamic_slice.18
  402.5 7.0 conditional.2
  403.1 0.6 compare_and_fusion
  403.7 0.8 constant_dynamic-slice_fusion
  405.0 1.0 constant_dynamic-slice_fusion.1
  406.0 0.8 copy.18
  407.2 1.8 reshape.110
  409.5 0.6 dynamic_slice.18
  411.4 7.0 conditional.2
  412.0 0.6 compare_and_fusion
  412.6 0.8 constant_dynamic-slice_fusion
  413.9 1.0 constant_dynamic-slice_fusion.1
  414.9 0.8 copy.18
  416.1 1.8 reshape.110
  420.2 7.0 conditional.2
  420.9 0.6 compare_and_fusion
  421.5 0.8 constant_dynamic-slice_fusion
  422.8 1.0 constant_dynamic-slice_fusion.1
  423.8 0.8 copy.18
  425.0 1.8 reshape.110
  451.9 0.6 dynamic_slice.18
  461.4 0.6 dynamic_slice.18
  488.0 0.6 dynamic_slice.18
  497.4 0.6 dynamic_slice.18
  524.0 0.6 dynamic_slice.18
  533.5 0.6 dynamic_slice.18
  543.2 1.2 fusion.28
  544.3 10.5 psum.7
  555.0 1.2 maximum_bitcast_fusion
  556.4 4.2 broadcast_in_dim.23
  560.6 432.2 %all-to-all-start.1 = ((bf16[64,256,256]{2,1,0:T(8,128)(2,1)}), bf16[64,256,256]{2,1,0:T(8,128)(2,1)}, u32[]{:S(2)}, u32[]{:S(2)}) async-start(bf16[64,256,256]{2,1,0:T(8,128)(2,1)} %bitcast.55), calls=%async_computation.1 | async-start | bytes 16777216 | tf_op jit(solution)/shard_map/all_to_all | solution.py:141
  992.8 186.1 %all-to-all-done.1 = bf16[64,256,256]{2,1,0:T(8,128)(2,1)} async-done(((bf16[64,256,256]{2,1,0:T(8,128)(2,1)}), bf16[64,256,256]{2,1,0:T(8,128)(2,1)}, u32[]{:S(2)}, u32[]{:S(2)}) %all-to-all-start.1) | async-done | bytes 8388640 | tf_op jit(solution)/shard_map/all_to_all | solution.py:141
  1178.9 9.2 fusion.47
  1188.1 8.0 fusion.11
  1196.2 8.8 fusion.25
  1205.0 16.5 %fusion.46 = (f32[512]{0:T(512)S(1)}, f32[512,16384]{0,1:T(8,128)}) fusion(bf16[512,128]{1,0:T(8,128)(2,1)S(1)} %bitcast.59, bf16[1,16384,256]{2,1,0:T(8,128)(2,1)} %bitcast.7, s32[512]{0:T(512)S(1)} %get-tuple-element.124), kind=kOutput, calls=%fused_computation.70 | convolution fusion | flops 2181037568 | bytes 37883904 | tf_op jit(solution)/shard_map/qd,kd->qk/dot_general | solution.py:45
  1221.5 15.0 %fusion.6 = f32[512]{0:T(512)S(1)} fusion(f32[512,16384]{0,1:T(8,128)} %get-tuple-element.120, f32[512]{0:T(512)S(1)} %get-tuple-element.119), kind=kLoop, calls=%fused_computation.14 | loop fusion | flops 16776704 | bytes 33558528 | tf_op jit(solution)/shard_map/reduce_sum | solution.py:51
  1236.5 14.9 %fusion.19 = bf16[512,128]{1,0:T(8,128)(2,1)S(1)} fusion(bf16[1,16384,256]{2,1,0:T(8,128)(2,1)} %bitcast.7, f32[512,16384]{0,1:T(8,128)} %get-tuple-element.120, f32[512]{0:T(512)S(1)} %get-tuple-element.119, f32[512]{0:T(512)S(1)} %fusion.6), kind=kOutput, calls=%fused_computation.30 | convolution fusion | flops 2164391936 | bytes 37883904 | tf_op jit(solution)/shard_map/dot_general | solution.py:52
  1251.4 0.7 maximum_bitcast_fusion.1
  (225 shorter events, 39.2 us)
Async XLA Ops:
  7.8 12.4 copy-start.2
  7.8 13.3 %copy-start.3 = (bf16[256,512]{1,0:T(8,128)(2,1)S(1)}, bf16[256,512]{1,0:T(8,128)(2,1)}, u32[]{:S(2)}) copy-start(bf16[256,512]{1,0:T(8,128)(2,1)} %param.15) | copy-start | bytes 786436
  7.8 14.0 %copy-start.4 = (bf16[16384,4]{0,1:T(4,128)(2,1)S(1)}, bf16[16384,4]{0,1:T(4,128)(2,1)}, u32[]{:S(2)}) copy-start(bf16[16384,4]{0,1:T(4,128)(2,1)} %param.13) | copy-start | bytes 393220
  7.8 381.2 %all-to-all-start = ((bf16[64,256,512]{1,2,0:T(8,128)(2,1)}), bf16[64,256,512]{1,2,0:T(8,128)(2,1)}, u32[]{:S(2)}, u32[]{:S(2)}) async-start(bf16[64,256,512]{1,2,0:T(8,128)(2,1)} %stack.2), calls=%async_computation | async-start | bytes 33554432 | tf_op jit(solution)/shard_map/all_to_all | solution.py:96
  389.0 167.3 %all-to-all-start.2 = ((bf16[64,16,128]{2,1,0:T(8,128)(2,1)}), bf16[64,16,128]{2,1,0:T(8,128)(2,1)S(1)}, u32[]{:S(2)}, u32[]{:S(2)}) async-start(bf16[64,16,128]{2,1,0:T(8,128)(2,1)} %bitcast.10), calls=%async_computation.2 | async-start | bytes 524288 | tf_op jit(solution)/shard_map/all_to_all | solution.py:140
  400.6 142.6 %copy-start = (bf16[256,512]{1,0:T(8,128)(2,1)S(1)}, bf16[256,512]{1,0:T(8,128)(2,1)}, u32[]{:S(2)}) copy-start(bf16[256,512]{1,0:T(8,128)(2,1)} %param.10) | copy-start | bytes 786436
  400.6 142.6 %copy-start.5 = (f32[512]{0:T(512)S(1)}, f32[512]{0:T(512)}, u32[]{:S(2)}) copy-start(f32[512]{0:T(512)} %param.12) | copy-start | bytes 6148
  544.3 643.8 %copy-start.1 = (bf16[256,512]{1,0:T(8,128)(2,1)}, bf16[256,512]{1,0:T(8,128)(2,1)S(1)}, u32[]{:S(2)}) copy-start(bf16[256,512]{1,0:T(8,128)(2,1)S(1)} %get-tuple-element.116) | copy-start | bytes 786436
  560.6 618.3 %all-to-all-start.1 = ((bf16[64,256,256]{2,1,0:T(8,128)(2,1)}), bf16[64,256,256]{2,1,0:T(8,128)(2,1)}, u32[]{:S(2)}, u32[]{:S(2)}) async-start(bf16[64,256,256]{2,1,0:T(8,128)(2,1)} %bitcast.55), calls=%async_computation.1 | async-start | bytes 16777216 | tf_op jit(solution)/shard_map/all_to_all | solution.py:141
